TPU v7x, 32 devices: a whole 2x2x4 slice. The times are simulated.
32 devices in a mesh: atm: 8 (over y, x, core), xg: 4 (over z).
Axes of the slice: x: 2, y: 2, z: 4, core: 2. Of those that a mesh axis runs over, the one named last changes fastest.
Arguments:
- fields_now: float32 [128, 48, 52, 128], P('atm', None, 'xg'), may hold values from -6 to 6
- upper: float32 [128, 48, 128], P(('atm', 'xg')), may hold values from 0.05 to 20
- lower: float32 [128, 48, 128], P(('atm', 'xg')), may hold values from 0.05 to 20
- surface_gain: float32 [128, 128], P(('atm', 'xg')), may hold values from 0.3 to 3
- route: int32 [8, 32, 2], P('atm'), may hold values from 0 to 16
- margin_slot: int32 [32, 96], P(('atm', 'xg')), may hold values from 0 to 15
- margin_block: int32 [32, 96], P(('atm', 'xg')), may hold values from 0 to 15
- margin_count: int32 [32], P(('atm', 'xg')), may hold values from 12 to 96, as said below
- margin_weight: float32 [32, 96, 128, 128], P(('atm', 'xg')), may hold values from 0 to 0.03
- surface_value: float32 [512, 52, 128], P(('atm', 'xg')), may hold values from -6 to 6
- exchange_coef: float32 [512, 128], P(('atm', 'xg')), may hold values from 0.05 to 2
- land_mask: int32 [512, 128], P(('atm', 'xg')), may hold values 0 or 1
- land_gain: float32 [512, 128], P(('atm', 'xg')), may hold values from 0.2 to 5
Outputs:
- fields_next: float32 [128, 48, 52, 128], P('atm', None, 'xg')
- surface_flux: float32 [512, 52, 128], P(('atm', 'xg'))
Inputs may be any that keep to these rules, and one draw needn't show every extreme that they name: `route`: the value 16 marks an empty slot; other values name a local column block of the sending atmosphere index. `margin_slot`: A value s names slot s % 2 from atmosphere index s // 2. `margin_count`: margins from this count on are padding; some owner has all 96 live.
All inputs are finite; a program needn't handle non-finite values. No bound on the sum of `land_mask` on one device may be relied on, other than what follows from the above.
Results may differ from a plain program's by a relative error of at most 0.0003.
Values sent between devices are 32-bit elements; how exact they have to be, the bound alone decides.
No kernel may reach another device: no remote copies, remote signals or barrier semaphores. Data moves between devices by JAX's collectives and lax.ppermute only.
A program may use at most 128 MiB of HBM per device.

v0:
```python
import jax
import jax.numpy as jnp
from jax import lax
from jax.sharding import PartitionSpec as P

HIGHEST = lax.Precision.HIGHEST


def factors(upper, lower):
    level_count = upper.shape[1]
    carried = jnp.zeros_like(upper[:, 0])
    inverses, multipliers, carries = ([], [], [])
    for height in range(level_count):
        from_above = upper[:, height] if height > 0 else jnp.zeros_like(carried)
        from_below = lower[:, height] if height < level_count - 1 else jnp.zeros_like(carried)
        inverse = 1.0 / (1.0 + from_above + from_below - from_above * carried)
        carried = from_below * inverse
        inverses.append(inverse)
        multipliers.append(from_above * inverse)
        carries.append(carried)
    return (jnp.stack(inverses, 1), jnp.stack(multipliers, 1), jnp.stack(carries, 1))


def per_device(
    fields_now,
    upper,
    lower,
    surface_gain,
    route,
    margin_slot,
    margin_block,
    margin_count,
    margin_weight,
    surface_value,
    exchange_coef,
    land_mask,
    land_gain,
):
    atm_count = lax.axis_size("atm")
    xg_count = lax.axis_size("xg")
    own_inverse, own_multiplier, own_carry = factors(upper, lower)
    own_bottom = surface_gain * own_inverse[:, -1]
    inverse, multiplier, carry_factor, bottom_gain = (
        lax.all_gather(own_inverse, "xg", axis=0, tiled=True),
        lax.all_gather(own_multiplier, "xg", axis=0, tiled=True),
        lax.all_gather(own_carry, "xg", axis=0, tiled=True),
        lax.all_gather(own_bottom, "xg", axis=0, tiled=True),
    )
    block_count = fields_now.shape[0]
    level_count = fields_now.shape[1]
    field_share = fields_now.shape[2]
    block_width = fields_now.shape[3]
    running = jnp.zeros_like(fields_now[:, 0])
    partials = []
    for height in range(level_count):
        running = (
            inverse[:, height, None, :] * fields_now[:, height]
            + multiplier[:, height, None, :] * running
        )
        partials.append(running)
    routing = route[0]
    pair_slots = routing.shape[1]
    quarter = block_width // xg_count
    send_value = jnp.concatenate(
        [running, jnp.zeros((1, field_share, block_width), jnp.float32)], 0
    )[routing]
    own_columns = lax.dynamic_slice_in_dim(bottom_gain, lax.axis_index("xg") * quarter, quarter, 1)
    send_gain = jnp.concatenate([own_columns, jnp.zeros((1, quarter), jnp.float32)], 0)[routing]
    got_value, got_gain = (
        lax.all_to_all(send_value, ("atm", "xg"), split_axis=0, concat_axis=0, tiled=True),
        lax.all_to_all(send_gain, ("atm", "xg"), split_axis=0, concat_axis=0, tiled=True),
    )
    got_value = got_value.reshape(atm_count, xg_count, pair_slots, field_share, block_width)
    got_gain = got_gain.reshape(atm_count, xg_count, pair_slots, quarter)
    slot_index = margin_slot[0]
    source = slot_index // pair_slots
    pair_index = slot_index % pair_slots
    margins = slot_index.shape[0]
    alive = (jnp.arange(margins, dtype=jnp.int32) < margin_count[0]).astype(jnp.float32)
    value_slots = got_value[source, :, pair_index].reshape(
        margins, xg_count * field_share, block_width
    )
    gain_slots = got_gain[source, :, pair_index].reshape(margins, block_width)
    weight = margin_weight[0]
    cell_blocks = surface_value.shape[0]
    select = (margin_block[0][None, :] == jnp.arange(cell_blocks, dtype=jnp.int32)[:, None]).astype(
        jnp.float32
    ) * alive[None, :]
    value_part = jnp.einsum("kxb,kfb->kfx", weight, value_slots, precision=HIGHEST)
    gain_part = jnp.einsum("kxb,kb->kx", weight, gain_slots, precision=HIGHEST)
    cell_value = jnp.einsum("jk,kfx->jfx", select, value_part, precision=HIGHEST)
    cell_gain = jnp.einsum("jk,kx->jx", select, gain_part, precision=HIGHEST)
    coupling = exchange_coef[:, None, :]
    land_total = land_mask.astype(jnp.float32) * land_gain
    surface_flux = (
        coupling
        * (surface_value - cell_value)
        / (1.0 + coupling * (cell_gain + land_total)[:, None, :])
    )
    returned = jnp.einsum("kxb,kfx->kfb", weight, surface_flux[margin_block[0]], precision=HIGHEST)
    returned = returned.reshape(margins, xg_count, field_share, block_width)
    by_source = (source[None, None, :] == jnp.arange(atm_count, dtype=jnp.int32)[:, None, None]) & (
        pair_index[None, None, :] == jnp.arange(pair_slots, dtype=jnp.int32)[None, :, None]
    )
    by_source = by_source.astype(jnp.float32) * alive[None, None, :]
    reply = jnp.einsum("apk,kgfb->agpfb", by_source, returned, precision=HIGHEST)
    answer = lax.all_to_all(
        reply.reshape(atm_count * xg_count, pair_slots, field_share, block_width),
        ("atm", "xg"),
        split_axis=0,
        concat_axis=0,
        tiled=True,
    )
    route_select = (
        routing[None, :, :] == jnp.arange(block_count, dtype=jnp.int32)[:, None, None]
    ).astype(jnp.float32)
    column_flux = jnp.einsum("rdp,dpfb->rfb", route_select, answer, precision=HIGHEST)
    state = running + bottom_gain[:, None, :] * column_flux
    outputs = [state]
    for height in range(level_count - 2, -1, -1):
        state = partials[height] + carry_factor[:, height, None, :] * state
        outputs.append(state)
    fields_next = jnp.stack(outputs[::-1], 1)
    return (fields_next, surface_flux)


def solution(mesh):
    in_specs = (
        P("atm", None, "xg", None),
        P(("atm", "xg"), None, None),
        P(("atm", "xg"), None, None),
        P(("atm", "xg"), None),
        P("atm", None, None),
        P(("atm", "xg"), None),
        P(("atm", "xg"), None),
        P(("atm", "xg")),
        P(("atm", "xg"), None, None, None),
        P(("atm", "xg"), None, None),
        P(("atm", "xg"), None),
        P(("atm", "xg"), None),
        P(("atm", "xg"), None),
    )
    out_specs = (P("atm", None, "xg", None), P(("atm", "xg"), None, None))
    return jax.shard_map(
        per_device, mesh=mesh, in_specs=in_specs, out_specs=out_specs, check_vma=False
    )
```

profile of v0, /device:TPU:0, one launch (start us, length us, event | category | flops | bytes accessed | tf_op | source)
XLA Modules:
  0.0 191.3 jit_solution(15118442074869055433)
XLA Ops:
  0.6 1.0 fusion.217
  1.6 1.2 fusion.213
  2.9 1.2 fusion.216
  4.1 1.2 fusion.218
  5.3 1.4 fusion.214
  6.7 1.2 fusion.215
  8.0 0.7 fusion.173
  8.6 0.7 compare_select_fusion
  9.5 1.3 multiply_bitcast_fusion
  10.8 13.6 %all-gather = f32[4,4,128]{2,1,0:T(4,128)S(1)} all-gather(f32[1,4,128]{2,1,0:T(4,128)S(1)} %get-tuple-element.36), channel_id=1, replica_groups=mesh['atm'=8,'xg'=4] {'xg'}, dimensions={0}, use_global_device_ids=true | all-gather | bytes 10240 | tf_op jit(solution)/shard_map/all_gather | solution.py:47
  25.1 1.2 gather_fusion.2
  26.3 4.3 %all-to-all-start.1 = ((f32[32,2,32]{2,1,0:T(2,128)}), f32[32,2,32]{2,1,0:T(2,128)S(1)}, u32[]{:S(2)}, u32[]{:S(2)}) async-start(f32[32,2,32]{2,1,0:T(2,128)} %bitcast.394), calls=%async_computation.1 | async-start | bytes 65536 | tf_op jit(solution)/shard_map/all_to_all | solution.py:71
  30.7 0.7 fusion.174
  31.3 0.7 and_select_fusion.1
  32.9 14.9 %all_gather.13 = f32[16,48,128]{2,1,0:T(8,128)S(1)} all-gather(f32[4,48,128]{2,1,0:T(8,128)S(1)} %copy.818), channel_id=1, replica_groups=mesh['atm'=8,'xg'=4] {'xg'}, dimensions={0}, use_global_device_ids=true | all-gather | bytes 491520 | tf_op jit(solution)/shard_map/all_gather | solution.py:45
  48.1 0.7 fusion.210
  49.1 15.5 %all_gather.12 = f32[16,48,128]{2,1,0:T(8,128)S(1)} all-gather(f32[4,48,128]{2,1,0:T(8,128)S(1)} %stack.412), channel_id=1, replica_groups=mesh['atm'=8,'xg'=4] {'xg'}, dimensions={0}, use_global_device_ids=true | all-gather | bytes 491520 | tf_op jit(solution)/shard_map/all_gather | solution.py:44
  64.6 0.7 fusion.211
  65.3 0.7 fusion.207
  66.0 0.7 fusion.209
  66.8 5.1 %fusion.203 = (f32[16,1,13,128]{3,1,2,0:T(1,128)S(1)}, f32[16,1,13,128]{3,1,2,0:T(1,128)S(1)}, f32[16,1,13,128]{3,1,2,0:T(1,128)S(1)}, f32[16,1,13,128]{3,1,2,0:...) fusion(f32[16,48,13,128]{3,1,2,0:T(8,128)} %param.13), kind=kLoop, calls=%fused_computation.526 | loop fusion | bytes 2129920 | tf_op jit(solution)/shard_map/slice | solution.py:57
  71.9 9.1 %fusion.202 = (f32[16,1,13,128]{3,1,2,0:T(1,128)S(1)}, f32[16,1,13,128]{3,1,2,0:T(1,128)S(1)}, f32[16,1,13,128]{3,1,2,0:T(1,128)S(1)}, f32[16,1,13,128]{3,1,2,0:...) fusion(f32[16,48,13,128]{3,1,2,0:T(8,128)} %param.13), kind=kLoop, calls=%fused_computation.525 | loop fusion | bytes 4046848 | tf_op jit(solution)/shard_map/slice | solution.py:57
  81.1 9.1 %fusion.201 = (f32[16,1,13,128]{3,1,2,0:T(1,128)S(1)}, f32[16,1,13,128]{3,1,2,0:T(1,128)S(1)}, f32[16,1,13,128]{3,1,2,0:T(1,128)S(1)}, f32[16,1,13,128]{3,1,2,0:...) fusion(f32[16,48,13,128]{3,1,2,0:T(8,128)} %param.13), kind=kLoop, calls=%fused_computation.524 | loop fusion | bytes 4046848 | tf_op jit(solution)/shard_map/slice | solution.py:57
  91.1 3.0 %fusion.24 = (f32[16,13,128]{2,0,1:T(8,128)S(1)}, f32[16,13,128]{2,0,1:T(8,128)S(1)}, f32[16,13,128]{2,0,1:T(8,128)S(1)}, f32[16,13,128]{2,0,1:T(8,128)S(1)}, f3...) fusion(f32[16,1,13,128]{3,1,2,0:T(1,128)S(1)} %get-tuple-elemen, ...), kind=kLoop, calls=%fused_computation.171 | loop fusion | flops 3807232 | bytes 8454144 | tf_op jit(solution)/shard_map/add | solution.py:57
  94.2 0.7 copy.819
  95.8 1.0 copy.869
  96.7 5.4 %all-to-all-start = ((f32[32,2,13,128]{3,1,2,0:T(2,128)}), f32[32,2,13,128]{3,1,2,0:T(2,128)S(1)}, u32[]{:S(2)}, u32[]{:S(2)}) async-start(f32[32,2,13,128]{3,1,2,0:T(2,128)} %copy.869), calls=%async_computation | async-start | bytes 851968 | tf_op jit(solution)/shard_map/all_to_all | solution.py:70
  102.1 1.2 gather_fusion.3
  103.5 11.8 %fusion.2 = f32[96,1,128]{2,1,0:T(1,128)S(1)} fusion(f32[96,128,1]{1,2,0:T(1,128)S(1)} %copy.884, f32[1,96,128,128]{3,2,1,0:T(8,128)} %param.21), kind=kOutput, calls=%fused_computation.7 | convolution fusion | flops 18874368 | bytes 6389760 | tf_op jit(solution)/shard_map/kxb,kb->kx/dot_general | solution.py:90
  115.7 2.8 %gather_fusion.1 = f32[96,4,13,128]{3,1,2,0:T(4,128)S(1)} fusion(f32[8,4,2,13,128]{4,1,3,2,0:T(4,128)S(1)} %copy.871, s32[96]{0:T(128)S(1)} %fusion.174), kind=kCustom, calls=%fused_computation.1 | custom fusion | bytes 5112576 | tf_op jit(solution)/shard_map/gather | solution.py:80
  118.8 16.4 %fusion.4 = f32[96,52,128]{2,1,0:T(8,128)S(1)} fusion(f32[1,96,128,128]{3,2,1,0:T(8,128)} %param.21, f32[96,52,128]{2,0,1:T(8,128)S(1)} %bitcast.1218), kind=kOutput, calls=%fused_computation.9 | convolution fusion | flops 981467136 | bytes 11403264 | tf_op jit(solution)/shard_map/kxb,kfb->kfx/dot_general | solution.py:89
  135.2 1.6 fusion.15
  137.6 0.8 gather_fusion.4
  138.4 7.8 %fusion = f32[96,52,128]{2,1,0:T(8,128)S(1)} fusion(f32[96,52,128]{2,1,0:T(8,128)S(1)} %gather_fusion.4, f32[1,96,128,128]{3,2,1,0:T(8,128)} %param.21), kind=kOutput, calls=%fused_computation.5 | convolution fusion | flops 981467136 | bytes 11403264 | tf_op jit(solution)/shard_map/kxb,kfx->kfb/dot_general | solution.py:100
  147.0 1.5 convolution_bitcast_fusion
  148.6 1.1 copy.881
  149.7 5.7 %all-to-all-start.2 = ((f32[32,2,13,128]{3,1,2,0:T(2,128)}), f32[32,2,13,128]{3,1,2,0:T(2,128)S(1)}, u32[]{:S(2)}, u32[]{:S(2)}) async-start(f32[32,2,13,128]{3,1,2,0:T(2,128)} %copy.881), calls=%async_computation.2 | async-start | bytes 851968 | tf_op jit(solution)/shard_map/all_to_all | solution.py:107
  155.4 21.2 %all_gather.14 = f32[16,48,128]{2,1,0:T(8,128)S(1)} all-gather(f32[4,48,128]{2,1,0:T(8,128)} %copy.819), channel_id=1, replica_groups=mesh['atm'=8,'xg'=4] {'xg'}, dimensions={0}, use_global_device_ids=true | all-gather | bytes 491520 | tf_op jit(solution)/shard_map/all_gather | solution.py:46
  176.6 0.7 fusion.206
  177.3 0.8 fusion.204
  178.1 0.8 fusion.205
  179.2 3.5 %constant_dynamic-update-slice_fusion.143 = (f32[16,48,13,128]{3,0,2,1:T(8,128)S(1)}, f32[16,13,128]{2,0,1:T(8,128)S(1)}, f32[16,13,128]{2,0,1:T(8,128)S(1)}, f3...) fusion(f32[16,1,13,128]{3,1,2,0:T(1,128)S(1)} %copy-done.32, ...), kind=kOutput, calls=%fused_computation.168 | convolution fusion | flops 24894464 | bytes 8986880 | tf_op jit(solution)/shard_map/rdp,dpfb->rfb/dot_general | solution.py:117
  182.8 0.7 constant_dynamic-update-slice_fusion.141
  183.6 0.7 constant_dynamic-update-slice_fusion.139
  184.4 0.7 constant_dynamic-update-slice_fusion.133
  185.1 0.7 constant_dynamic-update-slice_fusion.131
  185.9 0.7 constant_dynamic-update-slice_fusion.129
  187.4 3.9 %copy.883 = f32[16,48,13,128]{3,1,2,0:T(8,128)} copy(f32[16,48,13,128]{3,0,2,1:T(8,128)S(1)} %constant_dynamic-update-slice_fusion.96) | data formatting | bytes 10223616
  (294 shorter events, 5.9 us)
Async XLA Ops:
  26.3 70.4 %all-to-all-start.1 = ((f32[32,2,32]{2,1,0:T(2,128)}), f32[32,2,32]{2,1,0:T(2,128)S(1)}, u32[]{:S(2)}, u32[]{:S(2)}) async-start(f32[32,2,32]{2,1,0:T(2,128)} %bitcast.394), calls=%async_computation.1 | async-start | bytes 65536 | tf_op jit(solution)/shard_map/all_to_all | solution.py:71
  47.8 43.1 %copy-start.68 = (f32[16,1,128]{2,1,0:T(1,128)}, f32[16,1,128]{2,1,0:T(1,128)S(1)}, u32[]{:S(2)}) copy-start(f32[16,1,128]{2,1,0:T(1,128)S(1)} %get-tuple-element.321) | copy-start | bytes 24580
  47.9 43.1 %copy-start.69 = (f32[16,1,128]{2,1,0:T(1,128)}, f32[16,1,128]{2,1,0:T(1,128)S(1)}, u32[]{:S(2)}) copy-start(f32[16,1,128]{2,1,0:T(1,128)S(1)} %get-tuple-element.323) | copy-start | bytes 24580
  47.9 43.1 %copy-start.70 = (f32[16,1,128]{2,1,0:T(1,128)}, f32[16,1,128]{2,1,0:T(1,128)S(1)}, u32[]{:S(2)}) copy-start(f32[16,1,128]{2,1,0:T(1,128)S(1)} %get-tuple-element.325) | copy-start | bytes 24580
  47.9 43.1 %copy-start.71 = (f32[16,1,128]{2,1,0:T(1,128)}, f32[16,1,128]{2,1,0:T(1,128)S(1)}, u32[]{:S(2)}) copy-start(f32[16,1,128]{2,1,0:T(1,128)S(1)} %get-tuple-element.327) | copy-start | bytes 24580
  47.9 43.1 %copy-start.72 = (f32[16,1,128]{2,1,0:T(1,128)}, f32[16,1,128]{2,1,0:T(1,128)S(1)}, u32[]{:S(2)}) copy-start(f32[16,1,128]{2,1,0:T(1,128)S(1)} %get-tuple-element.328) | copy-start | bytes 24580
  47.9 43.1 %copy-start.73 = (f32[16,1,128]{2,1,0:T(1,128)}, f32[16,1,128]{2,1,0:T(1,128)S(1)}, u32[]{:S(2)}) copy-start(f32[16,1,128]{2,1,0:T(1,128)S(1)} %get-tuple-element.329) | copy-start | bytes 24580
  48.0 43.0 %copy-start.74 = (f32[16,1,128]{2,1,0:T(1,128)}, f32[16,1,128]{2,1,0:T(1,128)S(1)}, u32[]{:S(2)}) copy-start(f32[16,1,128]{2,1,0:T(1,128)S(1)} %get-tuple-element.256) | copy-start | bytes 24580
  48.0 43.0 %copy-start.75 = (f32[16,1,128]{2,1,0:T(1,128)}, f32[16,1,128]{2,1,0:T(1,128)S(1)}, u32[]{:S(2)}) copy-start(f32[16,1,128]{2,1,0:T(1,128)S(1)} %get-tuple-element.258) | copy-start | bytes 24580
  48.0 43.0 %copy-start.76 = (f32[16,1,128]{2,1,0:T(1,128)}, f32[16,1,128]{2,1,0:T(1,128)S(1)}, u32[]{:S(2)}) copy-start(f32[16,1,128]{2,1,0:T(1,128)S(1)} %get-tuple-element.260) | copy-start | bytes 24580
  48.1 43.0 %copy-start.77 = (f32[16,1,128]{2,1,0:T(1,128)}, f32[16,1,128]{2,1,0:T(1,128)S(1)}, u32[]{:S(2)}) copy-start(f32[16,1,128]{2,1,0:T(1,128)S(1)} %get-tuple-element.262) | copy-start | bytes 24580
  48.1 43.0 %copy-start.78 = (f32[16,1,128]{2,1,0:T(1,128)}, f32[16,1,128]{2,1,0:T(1,128)S(1)}, u32[]{:S(2)}) copy-start(f32[16,1,128]{2,1,0:T(1,128)S(1)} %get-tuple-element.264) | copy-start | bytes 24580
  48.1 43.0 %copy-start.79 = (f32[16,1,128]{2,1,0:T(1,128)}, f32[16,1,128]{2,1,0:T(1,128)S(1)}, u32[]{:S(2)}) copy-start(f32[16,1,128]{2,1,0:T(1,128)S(1)} %get-tuple-element.266) | copy-start | bytes 24580
  48.1 43.0 %copy-start.80 = (f32[16,1,128]{2,1,0:T(1,128)}, f32[16,1,128]{2,1,0:T(1,128)S(1)}, u32[]{:S(2)}) copy-start(f32[16,1,128]{2,1,0:T(1,128)S(1)} %get-tuple-element.268) | copy-start | bytes 24580
  48.1 43.0 %copy-start.81 = (f32[16,1,128]{2,1,0:T(1,128)}, f32[16,1,128]{2,1,0:T(1,128)S(1)}, u32[]{:S(2)}) copy-start(f32[16,1,128]{2,1,0:T(1,128)S(1)} %get-tuple-element.270) | copy-start | bytes 24580
  48.9 42.2 %copy-start.82 = (f32[16,1,128]{2,1,0:T(1,128)}, f32[16,1,128]{2,1,0:T(1,128)S(1)}, u32[]{:S(2)}) copy-start(f32[16,1,128]{2,1,0:T(1,128)S(1)} %get-tuple-element.291) | copy-start | bytes 24580
  71.8 22.3 %copy-start.23 = (f32[16,1,13,128]{3,1,2,0:T(1,128)}, f32[16,1,13,128]{3,1,2,0:T(1,128)S(1)}, u32[]{:S(2)}) copy-start(f32[16,1,13,128]{3,1,2,0:T(1,128)S(1)} %get-tuple-element.179) | copy-start | bytes 319492
  71.8 22.3 %copy-start.25 = (f32[16,1,13,128]{3,1,2,0:T(1,128)}, f32[16,1,13,128]{3,1,2,0:T(1,128)S(1)}, u32[]{:S(2)}) copy-start(f32[16,1,13,128]{3,1,2,0:T(1,128)S(1)} %get-tuple-element.181) | copy-start | bytes 319492
  71.9 22.3 %copy-start.27 = (f32[16,1,13,128]{3,1,2,0:T(1,128)}, f32[16,1,13,128]{3,1,2,0:T(1,128)S(1)}, u32[]{:S(2)}) copy-start(f32[16,1,13,128]{3,1,2,0:T(1,128)S(1)} %get-tuple-element.183) | copy-start | bytes 319492
  96.7 18.8 %all-to-all-start = ((f32[32,2,13,128]{3,1,2,0:T(2,128)}), f32[32,2,13,128]{3,1,2,0:T(2,128)S(1)}, u32[]{:S(2)}, u32[]{:S(2)}) async-start(f32[32,2,13,128]{3,1,2,0:T(2,128)} %copy.869), calls=%async_computation | async-start | bytes 851968 | tf_op jit(solution)/shard_map/all_to_all | solution.py:70
  146.2 32.6 %copy-start.1 = (f32[16,13,128]{2,0,1:T(8,128)S(1)}, f32[16,13,128]{2,0,1:T(8,128)}, u32[]{:S(2)}) copy-start(f32[16,13,128]{2,0,1:T(8,128)} %get-tuple-element.57) | copy-start | bytes 319492
  146.2 32.6 %copy-start.2 = (f32[16,13,128]{2,0,1:T(8,128)S(1)}, f32[16,13,128]{2,0,1:T(8,128)}, u32[]{:S(2)}) copy-start(f32[16,13,128]{2,0,1:T(8,128)} %get-tuple-element.58) | copy-start | bytes 319492
  146.3 32.6 %copy-start.3 = (f32[16,13,128]{2,0,1:T(8,128)S(1)}, f32[16,13,128]{2,0,1:T(8,128)}, u32[]{:S(2)}) copy-start(f32[16,13,128]{2,0,1:T(8,128)} %get-tuple-element.59) | copy-start | bytes 319492
  146.3 32.6 %copy-start.4 = (f32[16,13,128]{2,0,1:T(8,128)S(1)}, f32[16,13,128]{2,0,1:T(8,128)}, u32[]{:S(2)}) copy-start(f32[16,13,128]{2,0,1:T(8,128)} %get-tuple-element.60) | copy-start | bytes 319492
  146.3 32.6 %copy-start.5 = (f32[16,13,128]{2,0,1:T(8,128)S(1)}, f32[16,13,128]{2,0,1:T(8,128)}, u32[]{:S(2)}) copy-start(f32[16,13,128]{2,0,1:T(8,128)} %get-tuple-element.61) | copy-start | bytes 319492
  146.3 32.6 %copy-start.6 = (f32[16,13,128]{2,0,1:T(8,128)S(1)}, f32[16,13,128]{2,0,1:T(8,128)}, u32[]{:S(2)}) copy-start(f32[16,13,128]{2,0,1:T(8,128)} %get-tuple-element.62) | copy-start | bytes 319492
  146.3 32.6 %copy-start.7 = (f32[16,13,128]{2,0,1:T(8,128)S(1)}, f32[16,13,128]{2,0,1:T(8,128)}, u32[]{:S(2)}) copy-start(f32[16,13,128]{2,0,1:T(8,128)} %get-tuple-element.63) | copy-start | bytes 319492
  146.3 32.6 %copy-start.8 = (f32[16,13,128]{2,0,1:T(8,128)S(1)}, f32[16,13,128]{2,0,1:T(8,128)}, u32[]{:S(2)}) copy-start(f32[16,13,128]{2,0,1:T(8,128)} %get-tuple-element.64) | copy-start | bytes 319492
  146.3 32.6 %copy-start.9 = (f32[16,13,128]{2,0,1:T(8,128)S(1)}, f32[16,13,128]{2,0,1:T(8,128)}, u32[]{:S(2)}) copy-start(f32[16,13,128]{2,0,1:T(8,128)} %get-tuple-element.65) | copy-start | bytes 319492
  146.3 32.6 %copy-start.10 = (f32[16,13,128]{2,0,1:T(8,128)S(1)}, f32[16,13,128]{2,0,1:T(8,128)}, u32[]{:S(2)}) copy-start(f32[16,13,128]{2,0,1:T(8,128)} %get-tuple-element.66) | copy-start | bytes 319492
  146.3 32.6 %copy-start.11 = (f32[16,13,128]{2,0,1:T(8,128)S(1)}, f32[16,13,128]{2,0,1:T(8,128)}, u32[]{:S(2)}) copy-start(f32[16,13,128]{2,0,1:T(8,128)} %get-tuple-element.67) | copy-start | bytes 319492
  146.3 32.6 %copy-start.12 = (f32[16,13,128]{2,0,1:T(8,128)S(1)}, f32[16,13,128]{2,0,1:T(8,128)}, u32[]{:S(2)}) copy-start(f32[16,13,128]{2,0,1:T(8,128)} %get-tuple-element.68) | copy-start | bytes 319492
  146.4 32.6 %copy-start.13 = (f32[16,13,128]{2,0,1:T(8,128)S(1)}, f32[16,13,128]{2,0,1:T(8,128)}, u32[]{:S(2)}) copy-start(f32[16,13,128]{2,0,1:T(8,128)} %get-tuple-element.69) | copy-start | bytes 319492
  146.4 32.6 %copy-start.14 = (f32[16,13,128]{2,0,1:T(8,128)S(1)}, f32[16,13,128]{2,0,1:T(8,128)}, u32[]{:S(2)}) copy-start(f32[16,13,128]{2,0,1:T(8,128)} %get-tuple-element.70) | copy-start | bytes 319492
  146.4 32.6 %copy-start.15 = (f32[16,13,128]{2,0,1:T(8,128)S(1)}, f32[16,13,128]{2,0,1:T(8,128)}, u32[]{:S(2)}) copy-start(f32[16,13,128]{2,0,1:T(8,128)} %get-tuple-element.71) | copy-start | bytes 319492
  146.4 32.6 %copy-start.16 = (f32[16,13,128]{2,0,1:T(8,128)S(1)}, f32[16,13,128]{2,0,1:T(8,128)}, u32[]{:S(2)}) copy-start(f32[16,13,128]{2,0,1:T(8,128)} %get-tuple-element.72) | copy-start | bytes 319492
  146.4 32.6 %copy-start.17 = (f32[16,13,128]{2,0,1:T(8,128)S(1)}, f32[16,13,128]{2,0,1:T(8,128)}, u32[]{:S(2)}) copy-start(f32[16,13,128]{2,0,1:T(8,128)} %get-tuple-element.73) | copy-start | bytes 319492
  146.4 32.6 %copy-start.18 = (f32[16,13,128]{2,0,1:T(8,128)S(1)}, f32[16,13,128]{2,0,1:T(8,128)}, u32[]{:S(2)}) copy-start(f32[16,13,128]{2,0,1:T(8,128)} %get-tuple-element.74) | copy-start | bytes 319492
  146.4 32.6 %copy-start.19 = (f32[16,13,128]{2,0,1:T(8,128)S(1)}, f32[16,13,128]{2,0,1:T(8,128)}, u32[]{:S(2)}) copy-start(f32[16,13,128]{2,0,1:T(8,128)} %get-tuple-element.75) | copy-start | bytes 319492
  146.4 32.6 %copy-start.20 = (f32[16,13,128]{2,0,1:T(8,128)S(1)}, f32[16,13,128]{2,0,1:T(8,128)}, u32[]{:S(2)}) copy-start(f32[16,13,128]{2,0,1:T(8,128)} %get-tuple-element.76) | copy-start | bytes 319492
  146.4 32.6 %copy-start.22 = (f32[16,13,128]{2,0,1:T(8,128)S(1)}, f32[16,13,128]{2,0,1:T(8,128)}, u32[]{:S(2)}) copy-start(f32[16,13,128]{2,0,1:T(8,128)} %copy-done.21) | copy-start | bytes 319492
  146.4 32.6 %copy-start.24 = (f32[16,1,13,128]{3,1,2,0:T(1,128)S(1)}, f32[16,1,13,128]{3,1,2,0:T(1,128)}, u32[]{:S(2)}) copy-start(f32[16,1,13,128]{3,1,2,0:T(1,128)} %copy-done.23) | copy-start | bytes 319492
  146.5 32.6 %copy-start.26 = (f32[16,1,13,128]{3,1,2,0:T(1,128)S(1)}, f32[16,1,13,128]{3,1,2,0:T(1,128)}, u32[]{:S(2)}) copy-start(f32[16,1,13,128]{3,1,2,0:T(1,128)} %copy-done.25) | copy-start | bytes 319492
  146.5 32.6 %copy-start.28 = (f32[16,1,13,128]{3,1,2,0:T(1,128)S(1)}, f32[16,1,13,128]{3,1,2,0:T(1,128)}, u32[]{:S(2)}) copy-start(f32[16,1,13,128]{3,1,2,0:T(1,128)} %copy-done.27) | copy-start | bytes 319492
  146.5 32.6 %copy-start.30 = (f32[16,1,13,128]{3,1,2,0:T(1,128)S(1)}, f32[16,1,13,128]{3,1,2,0:T(1,128)}, u32[]{:S(2)}) copy-start(f32[16,1,13,128]{3,1,2,0:T(1,128)} %copy-done.29) | copy-start | bytes 319492
  146.5 32.6 %copy-start.32 = (f32[16,1,13,128]{3,1,2,0:T(1,128)S(1)}, f32[16,1,13,128]{3,1,2,0:T(1,128)}, u32[]{:S(2)}) copy-start(f32[16,1,13,128]{3,1,2,0:T(1,128)} %copy-done.31) | copy-start | bytes 319492
  146.5 32.6 %copy-start.86 = (s32[1,32,2]{1,2,0:T(2,128)S(1)}, s32[1,32,2]{1,2,0:T(2,128)}, u32[]{:S(2)}) copy-start(s32[1,32,2]{1,2,0:T(2,128)} %param.17) | copy-start | bytes 772
  149.7 29.1 %all-to-all-start.2 = ((f32[32,2,13,128]{3,1,2,0:T(2,128)}), f32[32,2,13,128]{3,1,2,0:T(2,128)S(1)}, u32[]{:S(2)}, u32[]{:S(2)}) async-start(f32[32,2,13,128]{3,1,2,0:T(2,128)} %copy.881), calls=%async_computation.2 | async-start | bytes 851968 | tf_op jit(solution)/shard_map/all_to_all | solution.py:107
  (43 other events, 395.1 us)
where the time goes:
time: 193 us; the launch traced here: 191 us
  blocking collectives  65.3 us (34%)
  local copies, waits for them, and re-layouts  52.7 us (27%)
  matrix products  42.8 us (22%)
  starting transfers between devices  15.4 us (8%)
  other arithmetic  11.8 us (6%)
  between operations  3.31 us (2%)
    slice x3, local copies, waits for them, and re-layouts, per_device(): fields_now[:, height]  23.2 us
    all_gather x1, blocking collectives, per_device(): lax.all_gather(own_carry, 'xg', axis=0, tiled=True)  21.2 us
    dot_general x1, matrix products, per_device(): jnp.einsum('kxb,kfb->kfx', weight, value_slots, precision=HIGHEST)  16.4 us
    all_gather x1, blocking collectives, per_device(): lax.all_gather(own_inverse, 'xg', axis=0, tiled=True)  15.5 us
    all_gather x1, blocking collectives, per_device(): lax.all_gather(own_multiplier, 'xg', axis=0, tiled=True)  14.9 us
    all_gather x1, blocking collectives, per_device(): lax.all_gather(own_bottom, 'xg', axis=0, tiled=True)  13.6 us
    dot_general x1, matrix products, per_device(): gain_part = jnp.einsum('kxb,kb->kx', weight, gain_slots, precision=HIGHEST)  11.8 us
    dot_general x1, matrix products, per_device(): jnp.einsum('kxb,kfx->kfb', weight, surface_flux[margin_block[0]], precisi...  7.85 us
  transfers between devices with their start and end apart: 3, of which 0 were waited for; matrix products, arithmetic and copies ran while one was open for 26% of the time, Pallas kernels for 0%

commit v1 on v0

--- a/solution.py
+++ b/solution.py
@@ -4,6 +4,18 @@
 from jax.sharding import PartitionSpec as P
 
 HIGHEST = lax.Precision.HIGHEST
+
+
+def doubled_up(x, axis, dim):
+    ways, here, hop = (lax.axis_size(axis), lax.axis_index(axis), x.shape[dim])
+    line, have = (x, 1)
+    while have < ways:
+        line = jnp.concatenate(
+            [line, lax.ppermute(line, axis, [(d, (d - have) % ways) for d in range(ways)])],
+            axis=dim,
+        )
+        have = 2 * have
+    return jnp.roll(line, here * hop, axis=dim)
 
 
 def factors(upper, lower):
@@ -44,7 +56,7 @@
         lax.all_gather(own_inverse, "xg", axis=0, tiled=True),
         lax.all_gather(own_multiplier, "xg", axis=0, tiled=True),
         lax.all_gather(own_carry, "xg", axis=0, tiled=True),
-        lax.all_gather(own_bottom, "xg", axis=0, tiled=True),
+        doubled_up(own_bottom, "xg", 0),
     )
     block_count = fields_now.shape[0]
     level_count = fields_now.shape[1]

time: 193 us -> 168 us (0.87)
  local copies, waits for them, and re-layouts: 52.7 us -> 33.9 us
  blocking collectives: 65.3 us -> 51.1 us
  waiting for transfers between devices: 0.01 us -> 8.09 us
    slice x3, local copies, waits for them, and re-layouts: 23.2 us -> 3.52 us  [per_device(): fields_now[:, height]]
    all_gather x1 -> x0, blocking collectives: 13.6 us -> none  [per_device(): lax.all_gather(own_bottom, 'xg', axis=0, tiled=True)]
    ppermute x0 -> x2, starting transfers between devices: none -> 5.89 us  [doubled_up(): lax.ppermute(line, axis, [(d, (d - have) % ways) for d in range(ways)])]
    all_to_all x1, waiting for transfers between devices: 0.01 us -> 4.92 us  [per_device(): lax.all_to_all(send_gain, ('atm', 'xg'), split_axis=0, concat_axis=0, til...]
    ppermute x0 -> x2, waiting for transfers between devices: none -> 3.15 us  [doubled_up(): lax.ppermute(line, axis, [(d, (d - have) % ways) for d in range(ways)])]
    all_to_all x1, starting transfers between devices: 5.35 us -> 2.78 us  [per_device(): lax.all_to_all(send_value, ('atm', 'xg'), split_axis=0, concat_axis=0, ti...]
    unnamed x201 -> x205, local copies, waits for them, and re-layouts: 5.72 us -> 5.51 us
  transfers between devices with their start and end apart: 3 -> 5, of which waited for: 0 -> 2; matrix products, arithmetic and copies ran while one was open for 26% -> 19% of each run, Pallas kernels for 0% -> 0%
where the time goes in v1:
time: 168 us; the launch traced here: 167 us
  blocking collectives  51.1 us (30%)
  matrix products  42.8 us (25%)
  local copies, waits for them, and re-layouts  33.9 us (20%)
  starting transfers between devices  17.3 us (10%)
  other arithmetic  10.7 us (6%)
  waiting for transfers between devices  8.09 us (5%)
  between operations  3.37 us (2%)
    all_gather x1, blocking collectives, per_device(): lax.all_gather(own_carry, 'xg', axis=0, tiled=True)  21.2 us
    dot_general x1, matrix products, per_device(): jnp.einsum('kxb,kfb->kfx', weight, value_slots, precision=HIGHEST)  16.4 us
    all_gather x1, blocking collectives, per_device(): lax.all_gather(own_multiplier, 'xg', axis=0, tiled=True)  15.1 us
    all_gather x1, blocking collectives, per_device(): lax.all_gather(own_inverse, 'xg', axis=0, tiled=True)  14.7 us
    dot_general x1, matrix products, per_device(): gain_part = jnp.einsum('kxb,kb->kx', weight, gain_slots, precision=HIGHEST)  11.8 us
    dot_general x1, matrix products, per_device(): jnp.einsum('kxb,kfx->kfb', weight, surface_flux[margin_block[0]], precisi...  7.85 us
    ppermute x2, starting transfers between devices, doubled_up(): lax.ppermute(line, axis, [(d, (d - have) % ways) for d in range(ways)])  5.89 us
    all_to_all x1, starting transfers between devices, per_device(): lax.all_to_all(reply.reshape(atm_count * xg_count, pair_slots, field_shar...  5.65 us
  transfers between devices with their start and end apart: 5, of which 2 were waited for; matrix products, arithmetic and copies ran while one was open for 19% of the time, Pallas kernels for 0%

profile of v1, /device:TPU:0, one launch (start us, length us, event | category | flops | bytes accessed | tf_op | source)
XLA Modules:
  0.0 167.2 jit_solution(4685497540422186497)
XLA Ops:
  0.6 1.0 fusion.216
  1.7 1.2 fusion.212
  2.9 1.2 fusion.215
  4.1 1.2 fusion.217
  5.3 1.4 fusion.213
  6.7 1.2 fusion.214
  8.0 1.3 fusion.176
  9.3 5.1 %collective-permute-start = (f32[4,128]{1,0:T(4,128)S(1)}, f32[4,128]{1,0:T(4,128)S(1)}, u32[]{:S(2)}, u32[]{:S(2)}) collective-permute-start(f32[4,128]{1,0:T(4,128)S(1)} %get-tuple-element.36), channel_id=1, source_target_pairs={{0,3},{1,0},{2,1},{3,2},{4,7},{5,4},{6,5},{7,6},{8,11},{9,8},{10,9... | collective-permute-start | bytes 6152 | tf_op jit(solution)/shard_map/ppermute | solution.py:14
  14.4 0.7 fusion.172
  16.7 15.1 %all_gather.10 = f32[16,48,128]{2,1,0:T(8,128)S(1)} all-gather(f32[4,48,128]{2,1,0:T(8,128)S(1)} %copy.726), channel_id=1, replica_groups=mesh['atm'=8,'xg'=4] {'xg'}, dimensions={0}, use_global_device_ids=true | all-gather | bytes 491520 | tf_op jit(solution)/shard_map/all_gather | solution.py:57
  32.1 0.7 fusion.209
  32.9 14.7 %all_gather.9 = f32[16,48,128]{2,1,0:T(8,128)S(1)} all-gather(f32[4,48,128]{2,1,0:T(8,128)S(1)} %copy.724), channel_id=1, replica_groups=mesh['atm'=8,'xg'=4] {'xg'}, dimensions={0}, use_global_device_ids=true | all-gather | bytes 491520 | tf_op jit(solution)/shard_map/all_gather | solution.py:56
  47.6 0.7 fusion.210
  48.3 0.7 fusion.206
  49.0 0.7 fusion.208
  49.8 0.7 fusion.202
  50.5 1.4 fusion.200
  52.0 1.4 fusion.201
  54.1 2.7 %fusion.22 = (f32[16,13,128]{2,0,1:T(8,128)S(1)}, f32[16,13,128]{2,0,1:T(8,128)S(1)}, f32[16,13,128]{2,0,1:T(8,128)S(1)}, f32[16,13,128]{2,0,1:T(8,128)}, f32[16...) fusion(f32[16,1,13,128]{3,1,2,0:T(1,128)S(1)} %get-tuple-elemen, ...), kind=kLoop, calls=%fused_computation.217 | loop fusion | flops 3807232 | bytes 8454144 | tf_op jit(solution)/shard_map/add | solution.py:69
  57.3 0.8 collective-permute-start.1
  58.7 3.2 %collective-permute-done.1 = f32[8,128]{1,0:T(8,128)S(1)} collective-permute-done((f32[8,128]{1,0:T(8,128)S(1)}, f32[8,128]{1,0:T(8,128)S(1)}, u32[]{:S(2)}, u32[]{:S(2)}) %collective-permute-start.1) | collective-permute-done | bytes 4128 | tf_op jit(solution)/shard_map/ppermute | solution.py:14
  62.0 1.2 gather_fusion.2
  63.2 2.9 %all-to-all-start.1 = ((f32[32,2,32]{2,1,0:T(2,128)}), f32[32,2,32]{2,1,0:T(2,128)S(1)}, u32[]{:S(2)}, u32[]{:S(2)}) async-start(f32[32,2,32]{2,1,0:T(2,128)} %bitcast.345), calls=%async_computation.1 | async-start | bytes 65536 | tf_op jit(solution)/shard_map/all_to_all | solution.py:83
  67.5 1.0 copy.777
  68.5 4.9 %all-to-all-done.1 = f32[32,2,32]{2,1,0:T(2,128)S(1)} async-done(((f32[32,2,32]{2,1,0:T(2,128)}), f32[32,2,32]{2,1,0:T(2,128)S(1)}, u32[]{:S(2)}, u32[]{:S(2)}) %all-to-all-start.1) | async-done | bytes 8224 | tf_op jit(solution)/shard_map/all_to_all | solution.py:83
  73.4 2.8 %all-to-all-start = ((f32[32,2,13,128]{3,1,2,0:T(2,128)}), f32[32,2,13,128]{3,1,2,0:T(2,128)S(1)}, u32[]{:S(2)}, u32[]{:S(2)}) async-start(f32[32,2,13,128]{3,1,2,0:T(2,128)} %copy.777), calls=%async_computation | async-start | bytes 851968 | tf_op jit(solution)/shard_map/all_to_all | solution.py:82
  76.7 1.2 gather_fusion.3
  78.1 11.8 %fusion.2 = f32[96,1,128]{2,1,0:T(1,128)S(1)} fusion(f32[96,128,1]{1,2,0:T(1,128)S(1)} %copy.792, f32[1,96,128,128]{3,2,1,0:T(8,128)} %param.21), kind=kOutput, calls=%fused_computation.7 | convolution fusion | flops 18874368 | bytes 6389760 | tf_op jit(solution)/shard_map/kxb,kb->kx/dot_general | solution.py:102
  90.3 2.8 %gather_fusion.1 = f32[96,4,13,128]{3,1,2,0:T(4,128)S(1)} fusion(f32[8,4,2,13,128]{4,1,3,2,0:T(4,128)S(1)} %copy.779, s32[96]{0:T(128)S(1)} %fusion.172), kind=kCustom, calls=%fused_computation.1 | custom fusion | bytes 5112576 | tf_op jit(solution)/shard_map/gather | solution.py:92
  93.4 16.4 %fusion.4 = f32[96,52,128]{2,1,0:T(8,128)S(1)} fusion(f32[1,96,128,128]{3,2,1,0:T(8,128)} %param.21, f32[96,52,128]{2,0,1:T(8,128)S(1)} %bitcast.1159), kind=kOutput, calls=%fused_computation.9 | convolution fusion | flops 981467136 | bytes 11403264 | tf_op jit(solution)/shard_map/kxb,kfb->kfx/dot_general | solution.py:101
  109.8 1.6 fusion.15
  112.2 0.8 gather_fusion.4
  113.0 7.9 %fusion = f32[96,52,128]{2,1,0:T(8,128)S(1)} fusion(f32[96,52,128]{2,1,0:T(8,128)S(1)} %gather_fusion.4, f32[1,96,128,128]{3,2,1,0:T(8,128)} %param.21), kind=kOutput, calls=%fused_computation.5 | convolution fusion | flops 981467136 | bytes 11403264 | tf_op jit(solution)/shard_map/kxb,kfx->kfb/dot_general | solution.py:112
  121.6 1.5 convolution_bitcast_fusion
  123.2 1.1 copy.789
  124.3 5.7 %all-to-all-start.2 = ((f32[32,2,13,128]{3,1,2,0:T(2,128)}), f32[32,2,13,128]{3,1,2,0:T(2,128)S(1)}, u32[]{:S(2)}, u32[]{:S(2)}) async-start(f32[32,2,13,128]{3,1,2,0:T(2,128)} %copy.789), calls=%async_computation.2 | async-start | bytes 851968 | tf_op jit(solution)/shard_map/all_to_all | solution.py:119
  130.0 21.2 %all_gather.11 = f32[16,48,128]{2,1,0:T(8,128)S(1)} all-gather(f32[4,48,128]{2,1,0:T(8,128)} %copy.727), channel_id=1, replica_groups=mesh['atm'=8,'xg'=4] {'xg'}, dimensions={0}, use_global_device_ids=true | all-gather | bytes 491520 | tf_op jit(solution)/shard_map/all_gather | solution.py:58
  151.2 0.7 fusion.205
  151.9 0.8 fusion.204
  152.7 0.7 fusion.203
  153.4 1.3 constant_dynamic-slice_fusion
  155.1 3.5 %constant_dynamic-update-slice_fusion.191 = (f32[16,48,13,128]{3,0,2,1:T(8,128)S(1)}, f32[16,13,128]{2,0,1:T(8,128)S(1)}, f32[16,13,128]{2,0,1:T(8,128)S(1)}, f3...) fusion(f32[16,1,13,128]{3,1,2,0:T(1,128)} %copy-done.33, ...), kind=kOutput, calls=%fused_computation.214 | convolution fusion | flops 24894464 | bytes 8986880 | tf_op jit(solution)/shard_map/rdp,dpfb->rfb/dot_general | solution.py:129
  158.7 0.8 constant_dynamic-update-slice_fusion.190
  159.4 0.7 constant_dynamic-update-slice_fusion.188
  160.2 0.7 constant_dynamic-update-slice_fusion.186
  160.9 0.7 constant_dynamic-update-slice_fusion.184
  161.7 0.7 constant_dynamic-update-slice_fusion.182
  163.3 3.9 %copy.791 = f32[16,48,13,128]{3,1,2,0:T(8,128)} copy(f32[16,48,13,128]{3,0,2,1:T(8,128)S(1)} %constant_dynamic-update-slice_fusion.144) | data formatting | bytes 10223616
  (304 shorter events, 7.4 us)
Async XLA Ops:
  0.6 49.1 %copy-start = (f32[16,48,13,128]{3,1,2,0:T(8,128)S(1)}, f32[16,48,13,128]{3,1,2,0:T(8,128)}, u32[]{:S(2)}) copy-start(f32[16,48,13,128]{3,1,2,0:T(8,128)} %param.13) | copy-start | bytes 15335428
  9.3 48.0 %collective-permute-start = (f32[4,128]{1,0:T(4,128)S(1)}, f32[4,128]{1,0:T(4,128)S(1)}, u32[]{:S(2)}, u32[]{:S(2)}) collective-permute-start(f32[4,128]{1,0:T(4,128)S(1)} %get-tuple-element.36), channel_id=1, source_target_pairs={{0,3},{1,0},{2,1},{3,2},{4,7},{5,4},{6,5},{7,6},{8,11},{9,8},{10,9... | collective-permute-start | bytes 6152 | tf_op jit(solution)/shard_map/ppermute | solution.py:14
  31.9 21.7 %copy-start.68 = (f32[16,1,128]{2,1,0:T(1,128)}, f32[16,1,128]{2,1,0:T(1,128)S(1)}, u32[]{:S(2)}) copy-start(f32[16,1,128]{2,1,0:T(1,128)S(1)} %get-tuple-element.318) | copy-start | bytes 24580
  31.9 21.7 %copy-start.69 = (f32[16,1,128]{2,1,0:T(1,128)}, f32[16,1,128]{2,1,0:T(1,128)S(1)}, u32[]{:S(2)}) copy-start(f32[16,1,128]{2,1,0:T(1,128)S(1)} %get-tuple-element.320) | copy-start | bytes 24580
  31.9 21.7 %copy-start.70 = (f32[16,1,128]{2,1,0:T(1,128)}, f32[16,1,128]{2,1,0:T(1,128)S(1)}, u32[]{:S(2)}) copy-start(f32[16,1,128]{2,1,0:T(1,128)S(1)} %get-tuple-element.322) | copy-start | bytes 24580
  31.9 21.7 %copy-start.71 = (f32[16,1,128]{2,1,0:T(1,128)}, f32[16,1,128]{2,1,0:T(1,128)S(1)}, u32[]{:S(2)}) copy-start(f32[16,1,128]{2,1,0:T(1,128)S(1)} %get-tuple-element.324) | copy-start | bytes 24580
  31.9 21.7 %copy-start.72 = (f32[16,1,128]{2,1,0:T(1,128)}, f32[16,1,128]{2,1,0:T(1,128)S(1)}, u32[]{:S(2)}) copy-start(f32[16,1,128]{2,1,0:T(1,128)S(1)} %get-tuple-element.326) | copy-start | bytes 24580
  31.9 21.7 %copy-start.73 = (f32[16,1,128]{2,1,0:T(1,128)}, f32[16,1,128]{2,1,0:T(1,128)S(1)}, u32[]{:S(2)}) copy-start(f32[16,1,128]{2,1,0:T(1,128)S(1)} %get-tuple-element.327) | copy-start | bytes 24580
  32.0 21.6 %copy-start.74 = (f32[16,1,128]{2,1,0:T(1,128)}, f32[16,1,128]{2,1,0:T(1,128)S(1)}, u32[]{:S(2)}) copy-start(f32[16,1,128]{2,1,0:T(1,128)S(1)} %get-tuple-element.253) | copy-start | bytes 24580
  32.1 21.6 %copy-start.75 = (f32[16,1,128]{2,1,0:T(1,128)}, f32[16,1,128]{2,1,0:T(1,128)S(1)}, u32[]{:S(2)}) copy-start(f32[16,1,128]{2,1,0:T(1,128)S(1)} %get-tuple-element.255) | copy-start | bytes 24580
  32.1 21.6 %copy-start.76 = (f32[16,1,128]{2,1,0:T(1,128)}, f32[16,1,128]{2,1,0:T(1,128)S(1)}, u32[]{:S(2)}) copy-start(f32[16,1,128]{2,1,0:T(1,128)S(1)} %get-tuple-element.257) | copy-start | bytes 24580
  32.1 21.6 %copy-start.77 = (f32[16,1,128]{2,1,0:T(1,128)}, f32[16,1,128]{2,1,0:T(1,128)S(1)}, u32[]{:S(2)}) copy-start(f32[16,1,128]{2,1,0:T(1,128)S(1)} %get-tuple-element.259) | copy-start | bytes 24580
  32.1 21.6 %copy-start.78 = (f32[16,1,128]{2,1,0:T(1,128)}, f32[16,1,128]{2,1,0:T(1,128)S(1)}, u32[]{:S(2)}) copy-start(f32[16,1,128]{2,1,0:T(1,128)S(1)} %get-tuple-element.261) | copy-start | bytes 24580
  32.1 21.6 %copy-start.79 = (f32[16,1,128]{2,1,0:T(1,128)}, f32[16,1,128]{2,1,0:T(1,128)S(1)}, u32[]{:S(2)}) copy-start(f32[16,1,128]{2,1,0:T(1,128)S(1)} %get-tuple-element.263) | copy-start | bytes 24580
  32.1 21.6 %copy-start.80 = (f32[16,1,128]{2,1,0:T(1,128)}, f32[16,1,128]{2,1,0:T(1,128)S(1)}, u32[]{:S(2)}) copy-start(f32[16,1,128]{2,1,0:T(1,128)S(1)} %get-tuple-element.265) | copy-start | bytes 24580
  57.3 4.6 %collective-permute-start.1 = (f32[8,128]{1,0:T(8,128)S(1)}, f32[8,128]{1,0:T(8,128)S(1)}, u32[]{:S(2)}, u32[]{:S(2)}) collective-permute-start(f32[8,128]{1,0:T(8,128)S(1)} %pad_maximum_fusion), channel_id=1, source_target_pairs={{0,2},{1,3},{2,0},{3,1},{4,6},{5,7},{6,4},{7,5},{8,10},{9,11},{10,... | collective-permute-start | bytes 12296 | tf_op jit(solution)/shard_map/ppermute | solution.py:14
  63.2 10.2 %all-to-all-start.1 = ((f32[32,2,32]{2,1,0:T(2,128)}), f32[32,2,32]{2,1,0:T(2,128)S(1)}, u32[]{:S(2)}, u32[]{:S(2)}) async-start(f32[32,2,32]{2,1,0:T(2,128)} %bitcast.345), calls=%async_computation.1 | async-start | bytes 65536 | tf_op jit(solution)/shard_map/all_to_all | solution.py:83
  66.8 23.1 %copy-start.84 = (f32[16,128]{1,0:T(8,128)S(1)}, f32[16,128]{1,0:T(8,128)}, u32[]{:S(2)}) copy-start(f32[16,128]{1,0:T(8,128)} %param.23) | copy-start | bytes 24580
  66.9 23.1 %copy-start.85 = (f32[16,128]{1,0:T(8,128)S(1)}, f32[16,128]{1,0:T(8,128)}, u32[]{:S(2)}) copy-start(f32[16,128]{1,0:T(8,128)} %param.25) | copy-start | bytes 24580
  66.9 23.1 %copy-start.86 = (s32[16,128]{1,0:T(8,128)S(1)}, s32[16,128]{1,0:T(8,128)}, u32[]{:S(2)}) copy-start(s32[16,128]{1,0:T(8,128)} %param.24) | copy-start | bytes 24580
  73.4 16.7 %all-to-all-start = ((f32[32,2,13,128]{3,1,2,0:T(2,128)}), f32[32,2,13,128]{3,1,2,0:T(2,128)S(1)}, u32[]{:S(2)}, u32[]{:S(2)}) async-start(f32[32,2,13,128]{3,1,2,0:T(2,128)} %copy.777), calls=%async_computation | async-start | bytes 851968 | tf_op jit(solution)/shard_map/all_to_all | solution.py:82
  120.8 33.9 %copy-start.2 = (f32[16,13,128]{2,0,1:T(8,128)S(1)}, f32[16,13,128]{2,0,1:T(8,128)}, u32[]{:S(2)}) copy-start(f32[16,13,128]{2,0,1:T(8,128)} %get-tuple-element.56) | copy-start | bytes 319492
  120.9 33.9 %copy-start.3 = (f32[16,13,128]{2,0,1:T(8,128)S(1)}, f32[16,13,128]{2,0,1:T(8,128)}, u32[]{:S(2)}) copy-start(f32[16,13,128]{2,0,1:T(8,128)} %get-tuple-element.57) | copy-start | bytes 319492
  120.9 33.9 %copy-start.4 = (f32[16,13,128]{2,0,1:T(8,128)S(1)}, f32[16,13,128]{2,0,1:T(8,128)}, u32[]{:S(2)}) copy-start(f32[16,13,128]{2,0,1:T(8,128)} %get-tuple-element.58) | copy-start | bytes 319492
  120.9 33.9 %copy-start.5 = (f32[16,13,128]{2,0,1:T(8,128)S(1)}, f32[16,13,128]{2,0,1:T(8,128)}, u32[]{:S(2)}) copy-start(f32[16,13,128]{2,0,1:T(8,128)} %get-tuple-element.59) | copy-start | bytes 319492
  120.9 33.9 %copy-start.6 = (f32[16,13,128]{2,0,1:T(8,128)S(1)}, f32[16,13,128]{2,0,1:T(8,128)}, u32[]{:S(2)}) copy-start(f32[16,13,128]{2,0,1:T(8,128)} %get-tuple-element.60) | copy-start | bytes 319492
  120.9 33.9 %copy-start.7 = (f32[16,13,128]{2,0,1:T(8,128)S(1)}, f32[16,13,128]{2,0,1:T(8,128)}, u32[]{:S(2)}) copy-start(f32[16,13,128]{2,0,1:T(8,128)} %get-tuple-element.61) | copy-start | bytes 319492
  120.9 33.9 %copy-start.8 = (f32[16,13,128]{2,0,1:T(8,128)S(1)}, f32[16,13,128]{2,0,1:T(8,128)}, u32[]{:S(2)}) copy-start(f32[16,13,128]{2,0,1:T(8,128)} %get-tuple-element.62) | copy-start | bytes 319492
  120.9 33.9 %copy-start.9 = (f32[16,13,128]{2,0,1:T(8,128)S(1)}, f32[16,13,128]{2,0,1:T(8,128)}, u32[]{:S(2)}) copy-start(f32[16,13,128]{2,0,1:T(8,128)} %get-tuple-element.63) | copy-start | bytes 319492
  120.9 33.9 %copy-start.10 = (f32[16,13,128]{2,0,1:T(8,128)S(1)}, f32[16,13,128]{2,0,1:T(8,128)}, u32[]{:S(2)}) copy-start(f32[16,13,128]{2,0,1:T(8,128)} %get-tuple-element.64) | copy-start | bytes 319492
  120.9 33.9 %copy-start.11 = (f32[16,13,128]{2,0,1:T(8,128)S(1)}, f32[16,13,128]{2,0,1:T(8,128)}, u32[]{:S(2)}) copy-start(f32[16,13,128]{2,0,1:T(8,128)} %get-tuple-element.65) | copy-start | bytes 319492
  120.9 33.9 %copy-start.12 = (f32[16,13,128]{2,0,1:T(8,128)S(1)}, f32[16,13,128]{2,0,1:T(8,128)}, u32[]{:S(2)}) copy-start(f32[16,13,128]{2,0,1:T(8,128)} %get-tuple-element.66) | copy-start | bytes 319492
  121.0 33.9 %copy-start.13 = (f32[16,13,128]{2,0,1:T(8,128)S(1)}, f32[16,13,128]{2,0,1:T(8,128)}, u32[]{:S(2)}) copy-start(f32[16,13,128]{2,0,1:T(8,128)} %get-tuple-element.67) | copy-start | bytes 319492
  121.0 33.9 %copy-start.14 = (f32[16,13,128]{2,0,1:T(8,128)S(1)}, f32[16,13,128]{2,0,1:T(8,128)}, u32[]{:S(2)}) copy-start(f32[16,13,128]{2,0,1:T(8,128)} %get-tuple-element.68) | copy-start | bytes 319492
  121.0 33.9 %copy-start.15 = (f32[16,13,128]{2,0,1:T(8,128)S(1)}, f32[16,13,128]{2,0,1:T(8,128)}, u32[]{:S(2)}) copy-start(f32[16,13,128]{2,0,1:T(8,128)} %get-tuple-element.69) | copy-start | bytes 319492
  121.0 33.9 %copy-start.16 = (f32[16,13,128]{2,0,1:T(8,128)S(1)}, f32[16,13,128]{2,0,1:T(8,128)}, u32[]{:S(2)}) copy-start(f32[16,13,128]{2,0,1:T(8,128)} %get-tuple-element.70) | copy-start | bytes 319492
  121.0 33.9 %copy-start.17 = (f32[16,13,128]{2,0,1:T(8,128)S(1)}, f32[16,13,128]{2,0,1:T(8,128)}, u32[]{:S(2)}) copy-start(f32[16,13,128]{2,0,1:T(8,128)} %get-tuple-element.71) | copy-start | bytes 319492
  121.0 33.9 %copy-start.18 = (f32[16,13,128]{2,0,1:T(8,128)S(1)}, f32[16,13,128]{2,0,1:T(8,128)}, u32[]{:S(2)}) copy-start(f32[16,13,128]{2,0,1:T(8,128)} %get-tuple-element.72) | copy-start | bytes 319492
  121.0 33.9 %copy-start.19 = (f32[16,13,128]{2,0,1:T(8,128)S(1)}, f32[16,13,128]{2,0,1:T(8,128)}, u32[]{:S(2)}) copy-start(f32[16,13,128]{2,0,1:T(8,128)} %get-tuple-element.73) | copy-start | bytes 319492
  121.0 33.9 %copy-start.20 = (f32[16,13,128]{2,0,1:T(8,128)S(1)}, f32[16,13,128]{2,0,1:T(8,128)}, u32[]{:S(2)}) copy-start(f32[16,13,128]{2,0,1:T(8,128)} %get-tuple-element.74) | copy-start | bytes 319492
  121.0 33.9 %copy-start.21 = (f32[16,13,128]{2,0,1:T(8,128)S(1)}, f32[16,13,128]{2,0,1:T(8,128)}, u32[]{:S(2)}) copy-start(f32[16,13,128]{2,0,1:T(8,128)} %get-tuple-element.75) | copy-start | bytes 319492
  121.0 33.9 %copy-start.22 = (f32[16,13,128]{2,0,1:T(8,128)S(1)}, f32[16,13,128]{2,0,1:T(8,128)}, u32[]{:S(2)}) copy-start(f32[16,13,128]{2,0,1:T(8,128)} %get-tuple-element.76) | copy-start | bytes 319492
  121.1 33.9 %copy-start.24 = (f32[16,1,13,128]{3,1,2,0:T(1,128)S(1)}, f32[16,1,13,128]{3,1,2,0:T(1,128)}, u32[]{:S(2)}) copy-start(f32[16,1,13,128]{3,1,2,0:T(1,128)} %copy-done.23) | copy-start | bytes 319492
  121.1 33.9 %copy-start.26 = (f32[16,1,13,128]{3,1,2,0:T(1,128)S(1)}, f32[16,1,13,128]{3,1,2,0:T(1,128)}, u32[]{:S(2)}) copy-start(f32[16,1,13,128]{3,1,2,0:T(1,128)} %copy-done.25) | copy-start | bytes 319492
  121.1 33.9 %copy-start.28 = (f32[16,1,13,128]{3,1,2,0:T(1,128)S(1)}, f32[16,1,13,128]{3,1,2,0:T(1,128)}, u32[]{:S(2)}) copy-start(f32[16,1,13,128]{3,1,2,0:T(1,128)} %copy-done.27) | copy-start | bytes 319492
  121.1 33.9 %copy-start.30 = (f32[16,1,13,128]{3,1,2,0:T(1,128)S(1)}, f32[16,1,13,128]{3,1,2,0:T(1,128)}, u32[]{:S(2)}) copy-start(f32[16,1,13,128]{3,1,2,0:T(1,128)} %copy-done.29) | copy-start | bytes 319492
  121.1 33.9 %copy-start.32 = (f32[16,1,13,128]{3,1,2,0:T(1,128)S(1)}, f32[16,1,13,128]{3,1,2,0:T(1,128)}, u32[]{:S(2)}) copy-start(f32[16,1,13,128]{3,1,2,0:T(1,128)} %copy-done.31) | copy-start | bytes 319492
  124.3 30.4 %all-to-all-start.2 = ((f32[32,2,13,128]{3,1,2,0:T(2,128)}), f32[32,2,13,128]{3,1,2,0:T(2,128)S(1)}, u32[]{:S(2)}, u32[]{:S(2)}) async-start(f32[32,2,13,128]{3,1,2,0:T(2,128)} %copy.789), calls=%async_computation.2 | async-start | bytes 851968 | tf_op jit(solution)/shard_map/all_to_all | solution.py:119
  (47 other events, 264.6 us)
